TPU v7x, 256 devices: a whole 4x4x8 slice. The times are simulated.
256 devices in a mesh: wide: 16 (over z_hi, x, core), col: 16 (over y, z_lo).
Axes of the slice: x: 4, y: 4, z: 8 (z_hi: 2, z_lo: 4; z = z_hi * 4 + z_lo), core: 2. Of those that a mesh axis runs over, the one named last changes fastest.
Arguments:
- adjoint: bfloat16 [32, 6144], P(None, ('wide', 'col')), may hold values from -6 to 6
- operator: bfloat16 [6144, 196608], P('wide', 'col'), may hold values from -0.109375 to 0.109375
- owner: int32 [196608], P(('col', 'wide')), may hold values from 0 to 196607, as said below
Outputs:
- junction_sums: float32 [32, 196608], P(None, ('col', 'wide'))
Inputs may be any that keep to these rules, and one draw needn't show every extreme that they name: Unknown j of device block b = j // 768 (blocks ordered col first, then wide) has owner j itself, or is a duplicate whose owner is an unknown in the lower half of a block of the same index of col; duplicates lie only in the upper half of a block and owners of duplicates are never duplicates. One block hands at most 16 duplicates to the blocks of any one index of wide, and this count is reached in every draw, by some block towards every index of wide and towards some index of wide from every block.
All inputs are finite; a program needn't handle non-finite values.
Results may differ from a plain program's by a relative error of at most 0.0003.
Values may be sent and summed in bfloat16 or wider, within the bound.
No kernel may reach another device: no remote copies, remote signals or barrier semaphores. Data moves between devices by JAX's collectives and lax.ppermute only.
A program may use at most 64 MiB of HBM per device.

v0:
```python
import jax
import jax.numpy as jnp
from jax import lax
from jax.sharding import PartitionSpec as P

CAP = 16


def local(adjoint, operator, owner):
    wide_count = lax.axis_size("wide")
    own_width = owner.shape[0]
    block_cols = operator.shape[1]
    sensors = adjoint.shape[0]
    partials = jnp.dot(
        lax.all_gather(adjoint, "col", axis=1, tiled=True),
        operator,
        preferred_element_type=jnp.float32,
    )
    col_base = lax.axis_index("col") * block_cols
    summed = lax.psum_scatter(partials, "wide", scatter_dimension=1, tiled=True)
    positions = jnp.arange(own_width, dtype=jnp.int32)
    global_cols = col_base + lax.axis_index("wide") * own_width + positions
    repeated = owner != global_cols
    target_peer = owner // own_width % wide_count
    target_place = owner % own_width
    peers = jnp.arange(wide_count, dtype=jnp.int32)
    marks = ((target_peer[:, None] == peers[None, :]) & repeated[:, None]).astype(jnp.int32)
    ranking = jnp.sum((jnp.cumsum(marks, axis=0) - marks) * marks, axis=1)
    slot_of = target_peer * CAP + ranking
    slot_ids = jnp.arange(wide_count * CAP, dtype=jnp.int32)
    chosen = (slot_of[:, None] == slot_ids[None, :]) & repeated[:, None]
    selector = chosen.astype(jnp.float32)
    outgoing = jnp.dot(
        summed, selector, precision=lax.Precision.HIGHEST, preferred_element_type=jnp.float32
    )
    place_sum = jnp.sum(chosen.astype(jnp.int32) * (target_place + 1)[:, None], axis=0) - 1
    outgoing = outgoing.reshape(sensors, wide_count, CAP)
    places = place_sum.astype(jnp.float32).reshape(1, wide_count, CAP)
    arrived, arrived_places = (
        lax.all_to_all(outgoing, "wide", split_axis=1, concat_axis=1, tiled=True),
        lax.all_to_all(places, "wide", split_axis=1, concat_axis=1, tiled=True),
    )
    flat_values = arrived.reshape(sensors, wide_count * CAP)
    landing = arrived_places.reshape(-1).astype(jnp.int32)
    receiver = (landing[:, None] == positions[None, :]).astype(jnp.float32)
    kept = summed * (1.0 - repeated.astype(jnp.float32))[None, :]
    added = jnp.dot(
        flat_values, receiver, precision=lax.Precision.HIGHEST, preferred_element_type=jnp.float32
    )
    return kept + added


def solution(mesh):
    return jax.shard_map(
        local,
        mesh=mesh,
        in_specs=(P(None, ("wide", "col")), P("wide", "col"), P(("col", "wide"))),
        out_specs=P(None, ("col", "wide")),
        check_vma=False,
    )
```

profile of v0, /device:TPU:1, one launch (start us, length us, event | category | flops | bytes accessed | tf_op | source)
XLA Modules:
  0.0 167.5 jit_solution(11518465624353053526)
XLA Ops:
  6.5 0.0 copy-start
  6.5 0.0 reduce-scatter.2.cloned.1.call-start
  6.5 38.5 %all_gather.3 = bf16[32,384]{0,1:T(8,128)(2,1)S(1)} all-gather(bf16[32,24]{0,1:T(8,128)(2,1)} %param.3), channel_id=1, replica_groups=mesh['wide'=16,'col'=16] {'col'}, dimensions={1}, use_global_device_ids=true | all-gather | bytes 26112 | tf_op jit(solution)/shard_map/all_gather | solution.py:15
  45.0 6.5 %fusion.15 = f32[32,12288]{1,0:T(8,128)} fusion(bf16[32,384]{0,1:T(8,128)(2,1)S(1)} %all_gather.3, bf16[384,12288]{1,0:T(8,128)(2,1)} %param.4), kind=kOutput, calls=%fused_computation.35 | convolution fusion | flops 301989888 | bytes 11034624 | tf_op jit(solution)/shard_map/dot_general | solution.py:14
  51.5 0.0 reduce-scatter.2.cloned.1.call-update
  51.5 0.0 copy-done
  51.6 1.7 %reduce-window.6 = s32[16,6,128]{2,0,1:T(8,128)S(1)} reduce-window(s32[16,6,128]{2,0,1:T(8,128)S(1)} %fusion.11, s32[]{:T(128)} %constant.48.clone.1), window={size=1x1x128 pad=0_0x0_0x127_0}, to_apply=%region_1.2 | reduce-window | flops 1560576 | bytes 98308 | tf_op jit(solution)/shard_map/reduce-window
  53.3 0.3 slice_reduce_fusion
  53.6 0.1 fusion.8
  53.7 0.7 select_reduce_fusion
  54.4 0.7 convert_element_type.40
  55.1 16.2 %all-to-all-start.1 = ((f32[1,16,16]{2,0,1:T(1,128)}), f32[1,16,16]{2,0,1:T(1,128)S(1)}, u32[]{:S(2)}, u32[]{:S(2)}) async-start(f32[1,16,16]{2,0,1:T(1,128)} %convert_element_type.40), calls=%async_computation.2 | async-start | bytes 16384 | tf_op jit(solution)/shard_map/all_to_all | solution.py:41
  71.2 67.5 %reduce-scatter.2.cloned.1.call-done = f32[32,768]{1,0:T(8,128)} async-done(((f32[32,12288]{1,0:T(8,128)}), f32[32,768]{1,0:T(8,128)}) %reduce-scatter.2.cloned.1.call-update) | async-done | bytes 98320 | tf_op jit(solution)/shard_map/reduce_scatter | solution.py:20
  138.8 1.9 %fusion.1 = f32[32,256]{0,1:T(8,128)S(1)} fusion(f32[32,768]{1,0:T(8,128)} %reduce-scatter.2.cloned.1.call-done, s32[768]{0:T(1024)S(1)} %multiply_add_fusion, pred[768]{0:T(1024)(128)(4,1)S(1)} %get-tuple-element.6), kind=kOutput, calls=%fused_computation.5 | convolution fusion | flops 75890688 | bytes 134912 | tf_op jit(solution)/shard_map/dot_general | solution.py:33
  140.7 0.7 reshape.65
  141.4 0.0 all-to-all-done.1
  141.4 6.2 %all-to-all-start = ((f32[16,1,512]{2,1,0:T(1,128)}), f32[16,1,512]{2,1,0:T(1,128)S(1)}, u32[]{:S(2)}, u32[]{:S(2)}) async-start(f32[16,1,512]{2,1,0:T(1,128)} %reshape.65), calls=%async_computation.1 | async-start | bytes 65536 | tf_op jit(solution)/shard_map/all_to_all | solution.py:40
  147.6 0.1 convert_element_type.42
  147.7 9.6 %all-to-all-done = f32[16,1,512]{2,1,0:T(1,128)S(1)} async-done(((f32[16,1,512]{2,1,0:T(1,128)}), f32[16,1,512]{2,1,0:T(1,128)S(1)}, u32[]{:S(2)}, u32[]{:S(2)}) %all-to-all-start) | async-done | bytes 32800 | tf_op jit(solution)/shard_map/all_to_all | solution.py:40
  157.3 0.5 broadcast.60
  157.8 0.7 reduce.6
  158.6 0.1 reshape.66
  158.6 2.0 %convolution_add_fusion = f32[32,768]{1,0:T(8,128)} fusion(f32[32,256]{0,1:T(8,128)S(1)} %bitcast.30, s32[256]{0:T(256)S(1)} %convert_element_type.42, f32[32,768]{1,0:T(8,128)} %reduce-scatter.2.cloned.1.call-done, f32[768]{0:T(1024)S(1)} %get-tuple-element.5), kind=kOutput, calls=%fused_computation | convolution fusion | flops 75743232 | bytes 233472 | tf_op jit(solution)/shard_map/dot_general | solution.py:47
  (7 shorter events, 0.1 us)
Async XLA Ops:
  6.5 45.0 %copy-start = (s32[768]{0:T(1024)S(1)}, s32[768]{0:T(1024)}, u32[]{:S(2)}) copy-start(s32[768]{0:T(1024)} %param.5) | copy-start | bytes 9220
  6.5 132.2 %reduce-scatter.2.cloned.1.call-start = ((), (), s32[]{:S(2)}) async-start(), calls=%async_computation.3 | async-start | bytes 1671168 | tf_op jit(solution)/shard_map/reduce_scatter | solution.py:20
  55.1 86.3 %all-to-all-start.1 = ((f32[1,16,16]{2,0,1:T(1,128)}), f32[1,16,16]{2,0,1:T(1,128)S(1)}, u32[]{:S(2)}, u32[]{:S(2)}) async-start(f32[1,16,16]{2,0,1:T(1,128)} %convert_element_type.40), calls=%async_computation.2 | async-start | bytes 16384 | tf_op jit(solution)/shard_map/all_to_all | solution.py:41
  141.4 15.9 %all-to-all-start = ((f32[16,1,512]{2,1,0:T(1,128)}), f32[16,1,512]{2,1,0:T(1,128)S(1)}, u32[]{:S(2)}, u32[]{:S(2)}) async-start(f32[16,1,512]{2,1,0:T(1,128)} %reshape.65), calls=%async_computation.1 | async-start | bytes 65536 | tf_op jit(solution)/shard_map/all_to_all | solution.py:40
Sparse Core Ops, SparseCore 0:
  51.6 87.0 reduce-scatter.1
where the time goes:
time: 168 us; the launch traced here: 167 us
  waiting for transfers between devices  77.2 us (46%)
  blocking collectives  38.5 us (23%)
  starting transfers between devices  22.3 us (13%)
  between operations  13.5 us (8%)
  matrix products  10.4 us (6%)
  other arithmetic  3.3 us (2%)
  local copies, waits for them, and re-layouts  2.36 us (1%)
    reduce_scatter x1, waiting for transfers between devices, local(): summed = lax.psum_scatter(partials, 'wide', scatter_dimension=1, tiled=True)  67.5 us
    all_gather x1, blocking collectives, local(): lax.all_gather(adjoint, 'col', axis=1, tiled=True)  38.5 us
    all_to_all x1, starting transfers between devices, local(): lax.all_to_all(places, 'wide', split_axis=1, concat_axis=1, tiled=True)  16.2 us
    all_to_all x1, waiting for transfers between devices, local(): lax.all_to_all(outgoing, 'wide', split_axis=1, concat_axis=1, tiled=True)  9.6 us
    dot_general x1, matrix products, local(): jnp.dot(lax.all_gather(adjoint, 'col', axis=1, tiled=True), operator, pre...  6.5 us
    all_to_all x1, starting transfers between devices, local(): lax.all_to_all(outgoing, 'wide', split_axis=1, concat_axis=1, tiled=True)  6.19 us
  transfers between devices with their start and end apart: 3, of which 2 were waited for; matrix products, arithmetic and copies ran while one was open for 4% of the time, Pallas kernels for 0%

commit v1 on v0

v1 whole, which is shorter than its diff:
```python
import functools

import jax
import jax.numpy as jnp
from jax import lax
from jax.experimental import pallas as pl
from jax.experimental.pallas import tpu as pltpu
from jax.sharding import PartitionSpec as P


CAP = 16
F32, BF16, I32 = jnp.float32, jnp.bfloat16, jnp.int32
VMEM = pl.BlockSpec(memory_space=pltpu.VMEM)
HBM = pl.BlockSpec(memory_space=pltpu.HBM)
COL_MASKS = (4, 12, 1, 2)
WIDE_MASKS = (1, 2, 6, 8)
GROUP = 4


def doubling_order(masks):
    order = [0]
    for mask in masks:
        order += [i ^ mask for i in order]
    return tuple(order)


def swap(value, axis, mask):
    count = lax.axis_size(axis)
    return lax.ppermute(value, axis, [(i, i ^ mask) for i in range(count)])


def prepare_kernel(peers, owner_hbm, adj_hbm, rows_ref, out_ref, owner_ref, sems):
    copies = [
        pltpu.make_async_copy(owner_hbm, owner_ref, sems.at[0]),
        pltpu.make_async_copy(adj_hbm, rows_ref, sems.at[1]),
    ]
    for copy in copies:
        copy.start()
    for copy in copies:
        copy.wait()
    lines, lane = owner_ref.shape
    width = lines * lane
    half = width // 2
    first = lax.axis_index("col") * (peers * width)
    parts = [owner_ref[i : i + 1] for i in range(lines // 2, lines)]
    owner = jnp.concatenate(parts, axis=1) - first
    own = lax.broadcasted_iota(I32, (1, half), 1) + (lax.axis_index("wide") * width + half)
    repeated = owner != own
    peer = owner // width
    place = owner - peer * width
    ids = lax.broadcasted_iota(I32, (peers, half), 0)
    marks = jnp.where((ids == peer) & repeated, 1.0, 0.0)
    rows = lax.broadcasted_iota(I32, (half, half), 0)
    columns = lax.broadcasted_iota(I32, (half, half), 1)
    earlier = jnp.where(rows < columns, 1.0, 0.0).astype(BF16)
    ahead = jnp.dot(marks.astype(BF16), earlier, preferred_element_type=F32)
    rank = jnp.sum(ahead * marks, axis=0, keepdims=True).astype(I32)
    out_ref[0, 0:1] = jnp.where(repeated, peer * CAP + rank, -1)
    out_ref[0, 1:2] = place_code(place)


def place_code(place):
    return jnp.where(place < 255, place + 1, 254 - place)


def adjoint_rows(order, pieces, rows_ref):
    me = lax.axis_index("col")
    depth, n = pieces[0].shape
    blocks = [piece[i : i + depth] for piece in pieces for i in range(0, piece.shape[0], depth)]
    for block, offset in zip(blocks, order):
        start = pl.multiple_of((me ^ offset) * depth, 8)
        rows_ref[pl.ds(start, depth), 0:n] = block.astype(F32)
    return rows_ref[:, 0:n].T.astype(BF16)


def operator_copies(targets, shift, op_ref, buf, sems):
    me = lax.axis_index("wide")
    half = buf.shape[2]

    def copy(i):
        start = pl.multiple_of((targets[i] ^ me) * (2 * half) + shift, 128)
        return pltpu.make_async_copy(op_ref.at[:, pl.ds(start, half)], buf.at[i], sems.at[i])

    for i in range(len(targets)):
        copy(i).start()
    return copy


def upper_kernel(blocks, order, *refs):
    *pieces, op_ref, keep_ref, send_ref, buf, rows_ref, sems = refs
    copy = operator_copies(range(blocks), buf.shape[2], op_ref, buf, sems)

    @pl.when(lax.axis_index("wide") >= 0)
    def _():
        adj = adjoint_rows(order, pieces, rows_ref)
        for first in range(0, blocks, GROUP):
            for j in range(first, first + GROUP):
                copy(j).wait()
            for j in range(first, first + GROUP):
                out = send_ref if j % 2 else keep_ref
                out[j // 2] = jnp.dot(adj, buf[j], preferred_element_type=F32)


def lower_blocks(targets, adj, slots, buf, keep_ref, send_ref):
    n = adj.shape[0]
    total, half = slots.shape[1], buf.shape[2]
    lanes = place_code(lax.broadcasted_iota(I32, (total, half), 1)).astype(F32).astype(BF16)
    for i in range(len(targets)):
        filled = slots[i]
        place = filled[:, 2 * n : 2 * n + 1]
        land = jnp.where(lanes == place, jnp.bfloat16(1), jnp.bfloat16(0))
        added = lax.dot_general(
            filled[:, 0 : 2 * n], land, (((0,), (0,)), ((), ())), preferred_element_type=F32
        )
        out = send_ref if i % 2 else keep_ref
        base = jnp.dot(adj, buf[i], preferred_element_type=F32)
        out[i // 2] = base + (added[0:n] + added[n : 2 * n])


def far_kernel(blocks, order, slot_order, codes_ref, up_keep_ref, up_send_ref, *refs):
    *pieces, op_ref, keep_ref, send_ref, near_slots, buf, rows_ref, slots, sems = refs
    targets = range(blocks // 2, blocks)
    copy = operator_copies(targets, 0, op_ref, buf, sems)
    half = buf.shape[2]
    n = up_keep_ref.shape[1]
    total = blocks * CAP

    @pl.when(lax.axis_index("wide") >= 0)
    def _():
        mine = lax.axis_index("wide") * CAP
        adj = adjoint_rows(order, pieces, rows_ref)
        ids = lax.broadcasted_iota(I32, (total, half), 0)
        for i, j in enumerate(slot_order):
            code = codes_ref[i]
            slot = jnp.where(code[0:1] < 0, -1, code[0:1] ^ mine)
            pick = jnp.where(ids == slot, 1.0, 0.0).astype(BF16)
            value = (up_send_ref if j % 2 else up_keep_ref)[j // 2]
            high = value.astype(BF16)
            low = (value - high.astype(F32)).astype(BF16)
            place = jnp.broadcast_to(code[1:2], (16, half)).astype(F32).astype(BF16)
            data = jnp.concatenate([high, low, place], axis=0)
            got = lax.dot_general(pick, data, (((1,), (1,)), ((), ())), preferred_element_type=F32)
            got = got.astype(BF16).reshape(blocks, CAP, 2 * n + 16)
            near_slots[:, j * CAP : (j + 1) * CAP, 0 : 2 * n + 16] = got[: blocks // 2]
            slots[:, j * CAP : (j + 1) * CAP, 0 : 2 * n + 16] = got[blocks // 2 :]
        for i in range(len(targets)):
            copy(i).wait()
        lower_blocks(targets, adj, slots, buf, keep_ref, send_ref)


def near_kernel(blocks, order, slots, *refs):
    *pieces, op_ref, keep_ref, send_ref, buf, rows_ref, sems = refs
    targets = range(blocks // 2)
    copy = operator_copies(targets, 0, op_ref, buf, sems)

    @pl.when(lax.axis_index("wide") >= 0)
    def _():
        adj = adjoint_rows(order, pieces, rows_ref)
        for i in range(len(targets)):
            copy(i).wait()
        lower_blocks(targets, adj, slots, buf, keep_ref, send_ref)


def half_products(kernel, count, operator, operands, half, extra=(), scratch=()):
    depth = operator.shape[0]
    n = operands[-1].shape[1]
    operator = pltpu.with_memory_space_constraint(operator, pltpu.HBM)
    shape = jax.ShapeDtypeStruct((count // 2, n, half), F32)
    return pl.pallas_call(
        kernel,
        out_shape=(shape, shape, *extra),
        in_specs=[VMEM] * len(operands) + [HBM],
        out_specs=(VMEM,) * (2 + len(extra)),
        scratch_shapes=[
            pltpu.VMEM((count, depth, half), operator.dtype),
            pltpu.VMEM((depth, 128), F32),
            *scratch,
            pltpu.SemaphoreType.DMA((count,)),
        ],
        compiler_params=pltpu.CompilerParams(vmem_limit_bytes=24 << 20),
    )(*operands, operator)


def program(adjoint, operator, owner):
    blocks = lax.axis_size("wide")
    lines = owner.shape[0] // 128
    half = owner.shape[0] // 2
    adj_t = adjoint.T
    rows, codes = pl.pallas_call(
        functools.partial(prepare_kernel, blocks),
        out_shape=(
            jax.ShapeDtypeStruct(adj_t.shape, adj_t.dtype),
            jax.ShapeDtypeStruct((1, 2, half), I32),
        ),
        in_specs=[HBM, HBM],
        out_specs=(VMEM, VMEM),
        scratch_shapes=[pltpu.VMEM((lines, 128), I32), pltpu.SemaphoreType.DMA((2,))],
        compiler_params=pltpu.CompilerParams(vmem_limit_bytes=4 << 20),
        name="prepare",
    )(
        pltpu.with_memory_space_constraint(owner.reshape(lines, 128), pltpu.HBM),
        pltpu.with_memory_space_constraint(adj_t, pltpu.HBM),
    )
    code = codes[0]
    pieces = [rows]
    for col_mask, wide_mask in zip(COL_MASKS, WIDE_MASKS):
        pieces.append(swap(jnp.concatenate(pieces, axis=0), "col", col_mask))
        codes_in = swap(codes, "wide", wide_mask)
        codes = jnp.concatenate([codes, codes_in], axis=0)
    order, slot_order = doubling_order(COL_MASKS), doubling_order(WIDE_MASKS)
    up_keep, up_send = half_products(
        functools.partial(upper_kernel, blocks, order), blocks, operator, pieces, half
    )
    slots = (blocks // 2, blocks * CAP, 128)
    far_keep, far_send, near_slots = half_products(
        functools.partial(far_kernel, blocks, order, slot_order),
        blocks // 2,
        operator,
        [codes, up_keep, up_send] + pieces,
        half,
        (jax.ShapeDtypeStruct(slots, BF16),),
        (pltpu.VMEM(slots, BF16),),
    )
    near_keep, near_send = half_products(
        functools.partial(near_kernel, blocks, order),
        blocks // 2,
        operator,
        [near_slots] + pieces,
        half,
    )
    upper = up_keep + swap(up_send, "wide", 1)
    far = far_keep + swap(far_send, "wide", 1)
    near = near_keep + swap(near_send, "wide", 1)
    far = jnp.stack([far, upper[4:]], axis=1)
    near = jnp.stack([near, upper[:4]], axis=1)
    r2 = swap(far[2:4], "wide", 6)
    t2 = swap(far[1] + r2[0], "wide", 2)
    across = swap(far[0] + r2[1] + t2, "wide", 8)
    r1 = swap(near[2:4], "wide", 6)
    t1 = swap(near[1] + r1[0], "wide", 2)
    total = near[0] + r1[1] + t1 + across
    return jnp.concatenate([total[0], jnp.where(code[0:1] >= 0, 0.0, total[1])], axis=1)


def solution(mesh):
    return jax.shard_map(
        program,
        mesh=mesh,
        in_specs=(P(None, ("wide", "col")), P("wide", "col"), P(("col", "wide"))),
        out_specs=P(None, ("col", "wide")),
        check_vma=False,
    )
```

time: 168 us -> 56.6 us (0.34)
  the two profiles are of different devices: /device:TPU:1 before, /device:TPU:36 now
where the time goes in v1:
time: 56.6 us; the launch traced here: 56.4 us
  starting transfers between devices  28.3 us (50%)
  waiting for transfers between devices  18.4 us (33%)
  Pallas kernels  8.65 us (15%)
  other arithmetic  0.92 us (2%)
    ppermute x16, starting transfers between devices, swap(): return lax.ppermute(value, axis, [(i, i ^ mask) for i in range(count)])  28.3 us
    ppermute x16, waiting for transfers between devices, swap(): return lax.ppermute(value, axis, [(i, i ^ mask) for i in range(count)])  18.4 us
    pallas_call x3, Pallas kernels, half_products(): pl.pallas_call(kernel, out_shape=(shape, shape, *extra), in_specs=[VMEM]...  7.74 us
  transfers between devices with their start and end apart: 16, of which 9 were waited for; matrix products, arithmetic and copies ran while one was open for 1% of the time, Pallas kernels for 9%

profile of v1, /device:TPU:36, one launch (start us, length us, event | category | flops | bytes accessed | tf_op | source)
XLA Modules:
  0.0 56.4 jit_solution(3430694061886827668)
XLA Ops:
  0.0 0.9 %prepare.1 = (bf16[24,32]{1,0:T(8,128)(2,1)S(1)}, s32[1,2,384]{2,1,0:T(2,128)S(1)}) custom-call(s32[6,128]{1,0:T(8,128)} %bitcast.41, bf16[24,32]{1,0:T(8,128)(2,1)} %bitcast.40), custom_call_target="tpu_custom_call" | custom-call | tf_op jit(solution)/shard_map/prepare/pallas_call | solution.py:189
  0.9 0.1 collective-permute-start
  1.0 1.7 %collective-permute-start.4 = (bf16[24,32]{1,0:T(8,128)(2,1)S(1)}, bf16[24,32]{1,0:T(8,128)(2,1)S(1)}, u32[]{:S(2)}, u32[]{:S(2)}) collective-permute-start(bf16[24,32]{1,0:T(8,128)(2,1)S(1)} %get-tuple-element.15.refs_0_), channel_id=1, source_target_pairs={{0,4},{1,5},{2,6},{3,7},{4,0},{5,1},{6,2},{7,3},{8,12},{9,13},{10,... | collective-permute-start | bytes 4616 | tf_op jit(solution)/shard_map/ppermute | solution.py:29
  2.7 2.1 %collective-permute-done.4.refs_1_ = bf16[24,32]{1,0:T(8,128)(2,1)S(1)} collective-permute-done((bf16[24,32]{1,0:T(8,128)(2,1)S(1)}, bf16[24,32]{1,0:T(8,128)(2,1)S(1)}, u32[]{:S(2)}, u32[]{:S(2)}) %collective-permute-start.4) | collective-permute-done | bytes 1568 | tf_op jit(solution)/shard_map/ppermute | solution.py:29
  4.7 3.0 %collective-permute-start.5 = (bf16[48,32]{1,0:T(8,128)(2,1)S(1)}, bf16[48,32]{1,0:T(8,128)(2,1)S(1)}, u32[]{:S(2)}, u32[]{:S(2)}) collective-permute-start(bf16[48,32]{1,0:T(8,128)(2,1)S(1)} %pad_maximum_fusion.5), channel_id=1, source_target_pairs={{0,12},{1,13},{2,14},{3,15},{4,8},{5,9},{6,10},{7,11},{8,4},{9,5},... | collective-permute-start | bytes 9224 | tf_op jit(solution)/shard_map/ppermute | solution.py:29
  7.8 0.0 collective-permute-done
  7.8 1.2 %collective-permute-start.1 = (s32[2,2,384]{2,1,0:T(2,128)S(1)}, s32[2,2,384]{2,1,0:T(2,128)S(1)}, u32[]{:S(2)}, u32[]{:S(2)}) collective-permute-start(s32[2,2,384]{2,1,0:T(2,128)S(1)} %pad_add_fusion.2), channel_id=1, source_target_pairs={{0,32},{16,48},{32,0},{48,16},{64,96},{80,112},{96,64},{112,80},{1... | collective-permute-start | bytes 18440 | tf_op jit(solution)/shard_map/ppermute | solution.py:29
  9.0 0.7 %collective-permute-done.5.refs_2_ = bf16[48,32]{1,0:T(8,128)(2,1)S(1)} collective-permute-done((bf16[48,32]{1,0:T(8,128)(2,1)S(1)}, bf16[48,32]{1,0:T(8,128)(2,1)S(1)}, u32[]{:S(2)}, u32[]{:S(2)}) %collective-permute-start.5) | collective-permute-done | bytes 3104 | tf_op jit(solution)/shard_map/ppermute | solution.py:29
  9.7 0.2 collective-permute-start.6
  9.9 1.5 %collective-permute-done.1 = s32[2,2,384]{2,1,0:T(2,128)S(1)} collective-permute-done((s32[2,2,384]{2,1,0:T(2,128)S(1)}, s32[2,2,384]{2,1,0:T(2,128)S(1)}, u32[]{:S(2)}, u32[]{:S(2)}) %collective-permute-start.1) | collective-permute-done | bytes 6176 | tf_op jit(solution)/shard_map/ppermute | solution.py:29
  11.4 0.5 collective-permute-start.2
  11.9 1.6 %collective-permute-done.6.refs_3_ = bf16[96,32]{1,0:T(8,128)(2,1)S(1)} collective-permute-done((bf16[96,32]{1,0:T(8,128)(2,1)S(1)}, bf16[96,32]{1,0:T(8,128)(2,1)S(1)}, u32[]{:S(2)}, u32[]{:S(2)}) %collective-permute-start.6) | collective-permute-done | bytes 6176 | tf_op jit(solution)/shard_map/ppermute | solution.py:29
  13.6 3.4 %collective-permute-start.7 = (bf16[192,32]{1,0:T(8,128)(2,1)S(1)}, bf16[192,32]{1,0:T(8,128)(2,1)S(1)}, u32[]{:S(2)}, u32[]{:S(2)}) collective-permute-start(bf16[192,32]{1,0:T(8,128)(2,1)S(1)} %pad_maximum_fusion.3), channel_id=1, source_target_pairs={{0,2},{1,3},{2,0},{3,1},{4,6},{5,7},{6,4},{7,5},{8,10},{9,11},{10,... | collective-permute-start | bytes 36872 | tf_op jit(solution)/shard_map/ppermute | solution.py:29
  16.9 0.0 collective-permute-done.2
  17.0 4.6 %collective-permute-start.3 = (s32[8,2,384]{2,1,0:T(2,128)S(1)}, s32[8,2,384]{2,1,0:T(2,128)S(1)}, u32[]{:S(2)}, u32[]{:S(2)}) collective-permute-start(s32[8,2,384]{2,1,0:T(2,128)S(1)} %pad_add_fusion), channel_id=1, source_target_pairs={{0,128},{16,144},{32,160},{48,176},{64,192},{80,208},{96,224},{112... | collective-permute-start | bytes 73736 | tf_op jit(solution)/shard_map/ppermute | solution.py:29
  21.6 0.0 collective-permute-done.7.refs_4_
  21.6 2.8 %shard_map.37 = (f32[8,32,384]{2,1,0:T(8,128)S(1)}, f32[8,32,384]{2,1,0:T(8,128)S(1)}) custom-call(bf16[24,32]{1,0:T(8,128)(2,1)S(1)} %get-tuple-element.15.refs_0_, bf16[24,32]{1,0:T(8,128)(2,1)S(1)} %collective-permute-done.4.refs_1_, bf16[48,32]{1,0:T(8,128)(2,1)S(1)} %collective-permute-done.5.refs_2_, ...), custom_call_target="tpu_custom_call" | custom-call | tf_op jit(solution)/shard_map/pallas_call | solution.py:169
  24.4 0.5 collective-permute-done.3
  24.8 2.5 %shard_map.38 = (f32[4,32,384]{2,1,0:T(8,128)S(1)}, f32[4,32,384]{2,1,0:T(8,128)S(1)}, bf16[8,256,128]{2,1,0:T(8,128)(2,1)S(1)}) custom-call(s32[16,2,384]{2,1,0:T(2,128)S(1)} %constant_dynamic-update-slice_fusion.codes_ref, f32[8,32,384]{2,1,0:T(8,128)S(1)} %get-tuple-element.16.up_keep_ref, f32[8,32,384]{2,1,0:T(8,128)S(1)} %get-tuple-element.17.up_send_ref, ...), custom_call_target="tpu_custom_call" | custom-call | tf_op jit(solution)/shard_map/pallas_call | solution.py:169
  27.3 0.1 collective-permute-start.12
  27.4 0.5 collective-permute-start.9
  27.9 2.5 %shard_map.39 = (f32[4,32,384]{2,1,0:T(8,128)S(1)}, f32[4,32,384]{2,1,0:T(8,128)S(1)}) custom-call(bf16[8,256,128]{2,1,0:T(8,128)(2,1)S(1)} %get-tuple-element.18.slots, bf16[24,32]{1,0:T(8,128)(2,1)S(1)} %get-tuple-element.15.refs_0_, bf16[24,32]{1,0:T(8,128)(2,1)S(1)} %collective-permute-done.4.refs_1_, bf16[48,32]{1,0:T(8,128)(2,1)S(1)} %collective-permute-done.5.refs_2_, ...), custom_call_target="tpu_custom_call" | custom-call | tf_op jit(solution)/shard_map/pallas_call | solution.py:169
  30.4 0.2 collective-permute-start.8
  30.6 0.0 collective-permute-done.12
  30.6 0.0 collective-permute-done.9
  30.7 0.6 %collective-permute-start.13 = (f32[2,2,32,384]{3,2,1,0:T(8,128)S(1)}, f32[2,2,32,384]{3,2,1,0:T(8,128)S(1)}, u32[]{:S(2)}, u32[]{:S(2)}) collective-permute-start(f32[2,2,32,384]{3,2,1,0:T(8,128)S(1)} %fusion), channel_id=1, source_target_pairs={{0,96},{16,112},{32,64},{48,80},{64,32},{80,48},{96,0},{112,16},{1... | collective-permute-start | bytes 589832 | tf_op jit(solution)/shard_map/ppermute | solution.py:29
  31.3 0.6 collective-permute-done.8
  32.0 1.0 %collective-permute-start.10 = (f32[2,2,32,384]{3,2,1,0:T(8,128)S(1)}, f32[2,2,32,384]{3,2,1,0:T(8,128)S(1)}, u32[]{:S(2)}, u32[]{:S(2)}) collective-permute-start(f32[2,2,32,384]{3,2,1,0:T(8,128)S(1)} %copy.23), channel_id=1, source_target_pairs={{0,96},{16,112},{32,64},{48,80},{64,32},{80,48},{96,0},{112,16},{1... | collective-permute-start | bytes 589832 | tf_op jit(solution)/shard_map/ppermute | solution.py:29
  33.0 5.6 %collective-permute-done.13 = f32[2,2,32,384]{3,2,1,0:T(8,128)S(1)} collective-permute-done((f32[2,2,32,384]{3,2,1,0:T(8,128)S(1)}, f32[2,2,32,384]{3,2,1,0:T(8,128)S(1)}, u32[]{:S(2)}, u32[]{:S(2)}) %collective-permute-start.13) | collective-permute-done | bytes 196640 | tf_op jit(solution)/shard_map/ppermute | solution.py:29
  38.6 3.1 %collective-permute-start.14 = (f32[2,32,384]{2,1,0:T(8,128)S(1)}, f32[2,32,384]{2,1,0:T(8,128)S(1)}, u32[]{:S(2)}, u32[]{:S(2)}) collective-permute-start(f32[2,32,384]{2,1,0:T(8,128)S(1)} %fusion.2), channel_id=1, source_target_pairs={{0,32},{16,48},{32,0},{48,16},{64,96},{80,112},{96,64},{112,80},{1... | collective-permute-start | bytes 294920 | tf_op jit(solution)/shard_map/ppermute | solution.py:29
  41.7 0.5 collective-permute-done.10
  42.3 3.1 %collective-permute-start.11 = (f32[2,32,384]{2,1,0:T(8,128)S(1)}, f32[2,32,384]{2,1,0:T(8,128)S(1)}, u32[]{:S(2)}, u32[]{:S(2)}) collective-permute-start(f32[2,32,384]{2,1,0:T(8,128)S(1)} %fusion.6), channel_id=1, source_target_pairs={{0,32},{16,48},{32,0},{48,16},{64,96},{80,112},{96,64},{112,80},{1... | collective-permute-start | bytes 294920 | tf_op jit(solution)/shard_map/ppermute | solution.py:29
  45.4 0.0 collective-permute-done.14
  45.4 5.0 %collective-permute-start.15 = (f32[2,32,384]{2,1,0:T(8,128)S(1)}, f32[2,32,384]{2,1,0:T(8,128)S(1)}, u32[]{:S(2)}, u32[]{:S(2)}) collective-permute-start(f32[2,32,384]{2,1,0:T(8,128)S(1)} %fusion.4), channel_id=1, source_target_pairs={{0,128},{16,144},{32,160},{48,176},{64,192},{80,208},{96,224},{112... | collective-permute-start | bytes 294920 | tf_op jit(solution)/shard_map/ppermute | solution.py:29
  50.4 0.0 collective-permute-done.11
  50.4 5.3 %collective-permute-done.15 = f32[2,32,384]{2,1,0:T(8,128)S(1)} collective-permute-done((f32[2,32,384]{2,1,0:T(8,128)S(1)}, f32[2,32,384]{2,1,0:T(8,128)S(1)}, u32[]{:S(2)}, u32[]{:S(2)}) %collective-permute-start.15) | collective-permute-done | bytes 98336 | tf_op jit(solution)/shard_map/ppermute | solution.py:29
  55.8 0.6 %pad_maximum_fusion.2 = f32[32,768]{1,0:T(8,128)} fusion(f32[32,384]{1,0:T(8,128)S(1)} %fusion.10, f32[32,384]{1,0:T(8,128)S(1)} %slice_bitcast_fusion.4), kind=kLoop, calls=%fused_computation.25 | loop fusion | flops 24576 | bytes 196608 | tf_op jit(solution)/shard_map/concatenate | solution.py:242
  (25 shorter events, 0.4 us)
Async XLA Ops:
  0.9 6.8 %collective-permute-start = (s32[1,2,384]{2,1,0:T(2,128)S(1)}, s32[1,2,384]{2,1,0:T(2,128)S(1)}, u32[]{:S(2)}, u32[]{:S(2)}) collective-permute-start(s32[1,2,384]{2,1,0:T(2,128)S(1)} %get-tuple-element.14), channel_id=1, source_target_pairs={{0,16},{16,0},{32,48},{48,32},{64,80},{80,64},{96,112},{112,96},{1... | collective-permute-start | bytes 9224 | tf_op jit(solution)/shard_map/ppermute | solution.py:29
  1.0 3.7 %collective-permute-start.4 = (bf16[24,32]{1,0:T(8,128)(2,1)S(1)}, bf16[24,32]{1,0:T(8,128)(2,1)S(1)}, u32[]{:S(2)}, u32[]{:S(2)}) collective-permute-start(bf16[24,32]{1,0:T(8,128)(2,1)S(1)} %get-tuple-element.15.refs_0_), channel_id=1, source_target_pairs={{0,4},{1,5},{2,6},{3,7},{4,0},{5,1},{6,2},{7,3},{8,12},{9,13},{10,... | collective-permute-start | bytes 4616 | tf_op jit(solution)/shard_map/ppermute | solution.py:29
  4.7 4.9 %collective-permute-start.5 = (bf16[48,32]{1,0:T(8,128)(2,1)S(1)}, bf16[48,32]{1,0:T(8,128)(2,1)S(1)}, u32[]{:S(2)}, u32[]{:S(2)}) collective-permute-start(bf16[48,32]{1,0:T(8,128)(2,1)S(1)} %pad_maximum_fusion.5), channel_id=1, source_target_pairs={{0,12},{1,13},{2,14},{3,15},{4,8},{5,9},{6,10},{7,11},{8,4},{9,5},... | collective-permute-start | bytes 9224 | tf_op jit(solution)/shard_map/ppermute | solution.py:29
  7.8 3.6 %collective-permute-start.1 = (s32[2,2,384]{2,1,0:T(2,128)S(1)}, s32[2,2,384]{2,1,0:T(2,128)S(1)}, u32[]{:S(2)}, u32[]{:S(2)}) collective-permute-start(s32[2,2,384]{2,1,0:T(2,128)S(1)} %pad_add_fusion.2), channel_id=1, source_target_pairs={{0,32},{16,48},{32,0},{48,16},{64,96},{80,112},{96,64},{112,80},{1... | collective-permute-start | bytes 18440 | tf_op jit(solution)/shard_map/ppermute | solution.py:29
  9.7 3.9 %collective-permute-start.6 = (bf16[96,32]{1,0:T(8,128)(2,1)S(1)}, bf16[96,32]{1,0:T(8,128)(2,1)S(1)}, u32[]{:S(2)}, u32[]{:S(2)}) collective-permute-start(bf16[96,32]{1,0:T(8,128)(2,1)S(1)} %pad_maximum_fusion.4), channel_id=1, source_target_pairs={{0,1},{1,0},{2,3},{3,2},{4,5},{5,4},{6,7},{7,6},{8,9},{9,8},{10,11... | collective-permute-start | bytes 18440 | tf_op jit(solution)/shard_map/ppermute | solution.py:29
  11.4 5.6 %collective-permute-start.2 = (s32[4,2,384]{2,1,0:T(2,128)S(1)}, s32[4,2,384]{2,1,0:T(2,128)S(1)}, u32[]{:S(2)}, u32[]{:S(2)}) collective-permute-start(s32[4,2,384]{2,1,0:T(2,128)S(1)} %pad_add_fusion.1), channel_id=1, source_target_pairs={{0,96},{16,112},{32,64},{48,80},{64,32},{80,48},{96,0},{112,16},{1... | collective-permute-start | bytes 36872 | tf_op jit(solution)/shard_map/ppermute | solution.py:29
  13.6 8.0 %collective-permute-start.7 = (bf16[192,32]{1,0:T(8,128)(2,1)S(1)}, bf16[192,32]{1,0:T(8,128)(2,1)S(1)}, u32[]{:S(2)}, u32[]{:S(2)}) collective-permute-start(bf16[192,32]{1,0:T(8,128)(2,1)S(1)} %pad_maximum_fusion.3), channel_id=1, source_target_pairs={{0,2},{1,3},{2,0},{3,1},{4,6},{5,7},{6,4},{7,5},{8,10},{9,11},{10,... | collective-permute-start | bytes 36872 | tf_op jit(solution)/shard_map/ppermute | solution.py:29
  17.0 7.8 %collective-permute-start.3 = (s32[8,2,384]{2,1,0:T(2,128)S(1)}, s32[8,2,384]{2,1,0:T(2,128)S(1)}, u32[]{:S(2)}, u32[]{:S(2)}) collective-permute-start(s32[8,2,384]{2,1,0:T(2,128)S(1)} %pad_add_fusion), channel_id=1, source_target_pairs={{0,128},{16,144},{32,160},{48,176},{64,192},{80,208},{96,224},{112... | collective-permute-start | bytes 73736 | tf_op jit(solution)/shard_map/ppermute | solution.py:29
  27.3 3.3 %collective-permute-start.12 = (f32[4,32,384]{2,1,0:T(8,128)S(1)}, f32[4,32,384]{2,1,0:T(8,128)S(1)}, u32[]{:S(2)}, u32[]{:S(2)}) collective-permute-start(f32[4,32,384]{2,1,0:T(8,128)S(1)} %get-tuple-element.22), channel_id=1, source_target_pairs={{0,16},{16,0},{32,48},{48,32},{64,80},{80,64},{96,112},{112,96},{1... | collective-permute-start | bytes 589832 | tf_op jit(solution)/shard_map/ppermute | solution.py:29
  27.4 3.2 %collective-permute-start.9 = (f32[8,32,384]{2,1,0:T(8,128)S(1)}, f32[8,32,384]{2,1,0:T(8,128)S(1)}, u32[]{:S(2)}, u32[]{:S(2)}) collective-permute-start(f32[8,32,384]{2,1,0:T(8,128)S(1)} %get-tuple-element.17.up_send_ref), channel_id=1, source_target_pairs={{0,16},{16,0},{32,48},{48,32},{64,80},{80,64},{96,112},{112,96},{1... | collective-permute-start | bytes 1179656 | tf_op jit(solution)/shard_map/ppermute | solution.py:29
  30.4 1.5 %collective-permute-start.8 = (f32[4,32,384]{2,1,0:T(8,128)S(1)}, f32[4,32,384]{2,1,0:T(8,128)S(1)}, u32[]{:S(2)}, u32[]{:S(2)}) collective-permute-start(f32[4,32,384]{2,1,0:T(8,128)S(1)} %get-tuple-element.20), channel_id=1, source_target_pairs={{0,16},{16,0},{32,48},{48,32},{64,80},{80,64},{96,112},{112,96},{1... | collective-permute-start | bytes 589832 | tf_op jit(solution)/shard_map/ppermute | solution.py:29
  30.7 7.9 %collective-permute-start.13 = (f32[2,2,32,384]{3,2,1,0:T(8,128)S(1)}, f32[2,2,32,384]{3,2,1,0:T(8,128)S(1)}, u32[]{:S(2)}, u32[]{:S(2)}) collective-permute-start(f32[2,2,32,384]{3,2,1,0:T(8,128)S(1)} %fusion), channel_id=1, source_target_pairs={{0,96},{16,112},{32,64},{48,80},{64,32},{80,48},{96,0},{112,16},{1... | collective-permute-start | bytes 589832 | tf_op jit(solution)/shard_map/ppermute | solution.py:29
  32.0 10.3 %collective-permute-start.10 = (f32[2,2,32,384]{3,2,1,0:T(8,128)S(1)}, f32[2,2,32,384]{3,2,1,0:T(8,128)S(1)}, u32[]{:S(2)}, u32[]{:S(2)}) collective-permute-start(f32[2,2,32,384]{3,2,1,0:T(8,128)S(1)} %copy.23), channel_id=1, source_target_pairs={{0,96},{16,112},{32,64},{48,80},{64,32},{80,48},{96,0},{112,16},{1... | collective-permute-start | bytes 589832 | tf_op jit(solution)/shard_map/ppermute | solution.py:29
  38.6 6.8 %collective-permute-start.14 = (f32[2,32,384]{2,1,0:T(8,128)S(1)}, f32[2,32,384]{2,1,0:T(8,128)S(1)}, u32[]{:S(2)}, u32[]{:S(2)}) collective-permute-start(f32[2,32,384]{2,1,0:T(8,128)S(1)} %fusion.2), channel_id=1, source_target_pairs={{0,32},{16,48},{32,0},{48,16},{64,96},{80,112},{96,64},{112,80},{1... | collective-permute-start | bytes 294920 | tf_op jit(solution)/shard_map/ppermute | solution.py:29
  42.3 8.2 %collective-permute-start.11 = (f32[2,32,384]{2,1,0:T(8,128)S(1)}, f32[2,32,384]{2,1,0:T(8,128)S(1)}, u32[]{:S(2)}, u32[]{:S(2)}) collective-permute-start(f32[2,32,384]{2,1,0:T(8,128)S(1)} %fusion.6), channel_id=1, source_target_pairs={{0,32},{16,48},{32,0},{48,16},{64,96},{80,112},{96,64},{112,80},{1... | collective-permute-start | bytes 294920 | tf_op jit(solution)/shard_map/ppermute | solution.py:29
  45.4 10.3 %collective-permute-start.15 = (f32[2,32,384]{2,1,0:T(8,128)S(1)}, f32[2,32,384]{2,1,0:T(8,128)S(1)}, u32[]{:S(2)}, u32[]{:S(2)}) collective-permute-start(f32[2,32,384]{2,1,0:T(8,128)S(1)} %fusion.4), channel_id=1, source_target_pairs={{0,128},{16,144},{32,160},{48,176},{64,192},{80,208},{96,224},{112... | collective-permute-start | bytes 294920 | tf_op jit(solution)/shard_map/ppermute | solution.py:29

commit v2 on v1

--- a/solution.py
+++ b/solution.py
@@ -15,6 +15,7 @@
 COL_MASKS = (4, 12, 1, 2)
 WIDE_MASKS = (1, 2, 6, 8)
 GROUP = 4
+LEVEL = 14.0
 
 
 def doubling_order(masks):
@@ -105,6 +106,7 @@
     n = adj.shape[0]
     total, half = slots.shape[1], buf.shape[2]
     lanes = place_code(lax.broadcasted_iota(I32, (total, half), 1)).astype(F32).astype(BF16)
+    largest = jnp.zeros((n, half), F32)
     for i in range(len(targets)):
         filled = slots[i]
         place = filled[:, 2 * n : 2 * n + 1]
@@ -114,10 +116,15 @@
         )
         out = send_ref if i % 2 else keep_ref
         base = jnp.dot(adj, buf[i], preferred_element_type=F32)
-        out[i // 2] = base + (added[0:n] + added[n : 2 * n])
-
-
-def far_kernel(blocks, order, slot_order, codes_ref, up_keep_ref, up_send_ref, *refs):
+        value = base + (added[0:n] + added[n : 2 * n])
+        out[i // 2] = value
+        largest = jnp.maximum(largest, jnp.abs(value))
+    return largest
+
+
+def far_kernel(blocks, order, slot_order, *refs):
+    count = len(WIDE_MASKS) + 1
+    codes, (up_keep_ref, up_send_ref), refs = refs[:count], refs[count : count + 2], refs[count + 2 :]
     *pieces, op_ref, keep_ref, send_ref, near_slots, buf, rows_ref, slots, sems = refs
     targets = range(blocks // 2, blocks)
     copy = operator_copies(targets, 0, op_ref, buf, sems)
@@ -130,11 +137,13 @@
         mine = lax.axis_index("wide") * CAP
         adj = adjoint_rows(order, pieces, rows_ref)
         ids = lax.broadcasted_iota(I32, (total, half), 0)
-        for i, j in enumerate(slot_order):
-            code = codes_ref[i]
+        code_rows = [ref[i] for ref in codes for i in range(ref.shape[0])]
+        largest = jnp.zeros((n, half), F32)
+        for code, j in zip(code_rows, slot_order):
             slot = jnp.where(code[0:1] < 0, -1, code[0:1] ^ mine)
             pick = jnp.where(ids == slot, 1.0, 0.0).astype(BF16)
             value = (up_send_ref if j % 2 else up_keep_ref)[j // 2]
+            largest = jnp.maximum(largest, jnp.abs(value))
             high = value.astype(BF16)
             low = (value - high.astype(F32)).astype(BF16)
             place = jnp.broadcast_to(code[1:2], (16, half)).astype(F32).astype(BF16)
@@ -145,7 +154,10 @@
             slots[:, j * CAP : (j + 1) * CAP, 0 : 2 * n + 16] = got[blocks // 2 :]
         for i in range(len(targets)):
             copy(i).wait()
-        lower_blocks(targets, adj, slots, buf, keep_ref, send_ref)
+        largest = jnp.maximum(largest, lower_blocks(targets, adj, slots, buf, keep_ref, send_ref))
+        largest = jnp.max(jnp.max(largest, axis=0, keepdims=True), axis=1, keepdims=True)
+        level = jnp.ceil(jnp.log2(jnp.maximum(largest, 2.0**-90))) + 1.0
+        send_ref[len(targets) // 2] = jnp.broadcast_to(level, (n, half))
 
 
 def near_kernel(blocks, order, slots, *refs):
@@ -161,14 +173,14 @@
         lower_blocks(targets, adj, slots, buf, keep_ref, send_ref)
 
 
-def half_products(kernel, count, operator, operands, half, extra=(), scratch=()):
+def half_products(kernel, count, operator, operands, half, extra=(), scratch=(), more=0):
     depth = operator.shape[0]
     n = operands[-1].shape[1]
     operator = pltpu.with_memory_space_constraint(operator, pltpu.HBM)
     shape = jax.ShapeDtypeStruct((count // 2, n, half), F32)
     return pl.pallas_call(
         kernel,
-        out_shape=(shape, shape, *extra),
+        out_shape=(shape, jax.ShapeDtypeStruct((count // 2 + more, n, half), F32), *extra),
         in_specs=[VMEM] * len(operands) + [HBM],
         out_specs=(VMEM,) * (2 + len(extra)),
         scratch_shapes=[
@@ -179,6 +191,18 @@
         ],
         compiler_params=pltpu.CompilerParams(vmem_limit_bytes=24 << 20),
     )(*operands, operator)
+
+
+def pack(value, level):
+    rows = value.reshape(-1, value.shape[-1])
+    scaled = (rows * jnp.exp2(LEVEL - level)).astype(jnp.float16)
+    return jnp.concatenate([scaled, jnp.broadcast_to(level, (16, rows.shape[1])).astype(jnp.float16)], axis=0)
+
+
+def unpack(message, shape):
+    rows = message.astype(F32)
+    level = rows[-1:]
+    return (rows[:-16] * jnp.exp2(level - LEVEL)).reshape(shape), level
 
 
 def program(adjoint, operator, owner):
@@ -202,11 +226,10 @@
         pltpu.with_memory_space_constraint(adj_t, pltpu.HBM),
     )
     code = codes[0]
-    pieces = [rows]
+    pieces, code_pieces = [rows], [codes]
     for col_mask, wide_mask in zip(COL_MASKS, WIDE_MASKS):
         pieces.append(swap(jnp.concatenate(pieces, axis=0), "col", col_mask))
-        codes_in = swap(codes, "wide", wide_mask)
-        codes = jnp.concatenate([codes, codes_in], axis=0)
+        code_pieces.append(swap(jnp.concatenate(code_pieces, axis=0), "wide", wide_mask))
     order, slot_order = doubling_order(COL_MASKS), doubling_order(WIDE_MASKS)
     up_keep, up_send = half_products(
         functools.partial(upper_kernel, blocks, order), blocks, operator, pieces, half
@@ -216,10 +239,11 @@
         functools.partial(far_kernel, blocks, order, slot_order),
         blocks // 2,
         operator,
-        [codes, up_keep, up_send] + pieces,
+        code_pieces + [up_keep, up_send] + pieces,
         half,
         (jax.ShapeDtypeStruct(slots, BF16),),
         (pltpu.VMEM(slots, BF16),),
+        more=1,
     )
     near_keep, near_send = half_products(
         functools.partial(near_kernel, blocks, order),
@@ -229,13 +253,20 @@
         half,
     )
     upper = up_keep + swap(up_send, "wide", 1)
-    far = far_keep + swap(far_send, "wide", 1)
+    far_in = swap(far_send, "wide", 1)
+    far = far_keep + far_in[:-1]
+    level = jnp.maximum(far_send[-1, 0:1], far_in[-1, 0:1]) + 1.0
     near = near_keep + swap(near_send, "wide", 1)
     far = jnp.stack([far, upper[4:]], axis=1)
     near = jnp.stack([near, upper[:4]], axis=1)
-    r2 = swap(far[2:4], "wide", 6)
-    t2 = swap(far[1] + r2[0], "wide", 2)
-    across = swap(far[0] + r2[1] + t2, "wide", 8)
+    message = swap(pack(far[2:4], level), "wide", 6)
+    r2, other = unpack(message, far[2:4].shape)
+    level = jnp.maximum(level, other) + 1.0
+    message = swap(pack(far[1] + r2[0], level), "wide", 2)
+    t2, other = unpack(message, far[1].shape)
+    level = jnp.maximum(level, other) + 1.0
+    message = swap(pack(far[0] + r2[1] + t2, level), "wide", 8)
+    across, other = unpack(message, far[0].shape)
     r1 = swap(near[2:4], "wide", 6)
     t1 = swap(near[1] + r1[0], "wide", 2)
     total = near[0] + r1[1] + t1 + across

time: 56.6 us -> 56 us (0.989)
  the two profiles are of different devices: /device:TPU:36 before, /device:TPU:6 now
where the time goes in v2:
time: 56 us; the launch traced here: 55.8 us
  waiting for transfers between devices  25 us (45%)
  starting transfers between devices  20.4 us (36%)
  Pallas kernels  8.75 us (16%)
  other arithmetic  1.32 us (2%)
    ppermute x16, waiting for transfers between devices, swap(): return lax.ppermute(value, axis, [(i, i ^ mask) for i in range(count)])  25 us
    ppermute x16, starting transfers between devices, swap(): return lax.ppermute(value, axis, [(i, i ^ mask) for i in range(count)])  20.4 us
    pallas_call x3, Pallas kernels, half_products(): pl.pallas_call(kernel, out_shape=(shape, jax.ShapeDtypeStruct((count // 2...  7.85 us
  transfers between devices with their start and end apart: 16, of which 11 were waited for; matrix products, arithmetic and copies ran while one was open for 1% of the time, Pallas kernels for 5%

profile of v2, /device:TPU:6, one launch (start us, length us, event | category | flops | bytes accessed | tf_op | source)
XLA Modules:
  0.0 55.8 jit_solution(18246543011929975719)
XLA Ops:
  0.0 0.9 %prepare.1 = (bf16[24,32]{1,0:T(8,128)(2,1)S(1)}, s32[1,2,384]{2,1,0:T(2,128)S(1)}) custom-call(s32[6,128]{1,0:T(8,128)} %bitcast.50, bf16[24,32]{1,0:T(8,128)(2,1)} %bitcast.49), custom_call_target="tpu_custom_call" | custom-call | tf_op jit(solution)/shard_map/prepare/pallas_call | solution.py:213
  0.9 0.1 collective-permute-start
  1.0 1.7 %collective-permute-start.4 = (bf16[24,32]{1,0:T(8,128)(2,1)S(1)}, bf16[24,32]{1,0:T(8,128)(2,1)S(1)}, u32[]{:S(2)}, u32[]{:S(2)}) collective-permute-start(bf16[24,32]{1,0:T(8,128)(2,1)S(1)} %get-tuple-element.15.refs_0_.refs_7_), channel_id=1, source_target_pairs={{0,4},{1,5},{2,6},{3,7},{4,0},{5,1},{6,2},{7,3},{8,12},{9,13},{10,... | collective-permute-start | bytes 4616 | tf_op jit(solution)/shard_map/ppermute | solution.py:30
  2.7 0.0 collective-permute-done.refs_1_
  2.7 0.8 %collective-permute-start.1 = (s32[2,2,384]{2,1,0:T(2,128)S(1)}, s32[2,2,384]{2,1,0:T(2,128)S(1)}, u32[]{:S(2)}, u32[]{:S(2)}) collective-permute-start(s32[2,2,384]{2,1,0:T(2,128)S(1)} %pad_add_fusion.2), channel_id=1, source_target_pairs={{0,32},{16,48},{32,0},{48,16},{64,96},{80,112},{96,64},{112,80},{1... | collective-permute-start | bytes 18440 | tf_op jit(solution)/shard_map/ppermute | solution.py:30
  3.5 1.2 %collective-permute-done.4.refs_1_.refs_8_ = bf16[24,32]{1,0:T(8,128)(2,1)S(1)} collective-permute-done((bf16[24,32]{1,0:T(8,128)(2,1)S(1)}, bf16[24,32]{1,0:T(8,128)(2,1)S(1)}, u32[]{:S(2)}, u32[]{:S(2)}) %collective-permute-start.4) | collective-permute-done | bytes 1568 | tf_op jit(solution)/shard_map/ppermute | solution.py:30
  4.7 3.0 %collective-permute-start.5 = (bf16[48,32]{1,0:T(8,128)(2,1)S(1)}, bf16[48,32]{1,0:T(8,128)(2,1)S(1)}, u32[]{:S(2)}, u32[]{:S(2)}) collective-permute-start(bf16[48,32]{1,0:T(8,128)(2,1)S(1)} %pad_maximum_fusion.9), channel_id=1, source_target_pairs={{0,12},{1,13},{2,14},{3,15},{4,8},{5,9},{6,10},{7,11},{8,4},{9,5},... | collective-permute-start | bytes 9224 | tf_op jit(solution)/shard_map/ppermute | solution.py:30
  7.8 0.0 collective-permute-done.1.refs_2_
  7.8 0.5 collective-permute-start.2
  8.2 1.4 %collective-permute-done.5.refs_2_.refs_9_ = bf16[48,32]{1,0:T(8,128)(2,1)S(1)} collective-permute-done((bf16[48,32]{1,0:T(8,128)(2,1)S(1)}, bf16[48,32]{1,0:T(8,128)(2,1)S(1)}, u32[]{:S(2)}, u32[]{:S(2)}) %collective-permute-start.5) | collective-permute-done | bytes 3104 | tf_op jit(solution)/shard_map/ppermute | solution.py:30
  9.7 2.0 %collective-permute-start.6 = (bf16[96,32]{1,0:T(8,128)(2,1)S(1)}, bf16[96,32]{1,0:T(8,128)(2,1)S(1)}, u32[]{:S(2)}, u32[]{:S(2)}) collective-permute-start(bf16[96,32]{1,0:T(8,128)(2,1)S(1)} %pad_maximum_fusion.8), channel_id=1, source_target_pairs={{0,1},{1,0},{2,3},{3,2},{4,5},{5,4},{6,7},{7,6},{8,9},{9,8},{10,11... | collective-permute-start | bytes 18440 | tf_op jit(solution)/shard_map/ppermute | solution.py:30
  11.7 1.0 %collective-permute-done.2.refs_3_ = s32[4,2,384]{2,1,0:T(2,128)S(1)} collective-permute-done((s32[4,2,384]{2,1,0:T(2,128)S(1)}, s32[4,2,384]{2,1,0:T(2,128)S(1)}, u32[]{:S(2)}, u32[]{:S(2)}) %collective-permute-start.2) | collective-permute-done | bytes 12320 | tf_op jit(solution)/shard_map/ppermute | solution.py:30
  12.7 7.2 %collective-permute-start.3 = (s32[8,2,384]{2,1,0:T(2,128)S(1)}, s32[8,2,384]{2,1,0:T(2,128)S(1)}, u32[]{:S(2)}, u32[]{:S(2)}) collective-permute-start(s32[8,2,384]{2,1,0:T(2,128)S(1)} %pad_add_fusion), channel_id=1, source_target_pairs={{0,128},{16,144},{32,160},{48,176},{64,192},{80,208},{96,224},{112... | collective-permute-start | bytes 73736 | tf_op jit(solution)/shard_map/ppermute | solution.py:30
  19.9 0.0 collective-permute-done.6.refs_3_.refs_10_
  19.9 1.6 %collective-permute-start.7 = (bf16[192,32]{1,0:T(8,128)(2,1)S(1)}, bf16[192,32]{1,0:T(8,128)(2,1)S(1)}, u32[]{:S(2)}, u32[]{:S(2)}) collective-permute-start(bf16[192,32]{1,0:T(8,128)(2,1)S(1)} %pad_maximum_fusion.7), channel_id=1, source_target_pairs={{0,2},{1,3},{2,0},{3,1},{4,6},{5,7},{6,4},{7,5},{8,10},{9,11},{10,... | collective-permute-start | bytes 36872 | tf_op jit(solution)/shard_map/ppermute | solution.py:30
  21.5 3.5 %collective-permute-done.7.refs_4_.refs_11_ = bf16[192,32]{1,0:T(8,128)(2,1)S(1)} collective-permute-done((bf16[192,32]{1,0:T(8,128)(2,1)S(1)}, bf16[192,32]{1,0:T(8,128)(2,1)S(1)}, u32[]{:S(2)}, u32[]{:S(2)}) %collective-permute-start.7) | collective-permute-done | bytes 12320 | tf_op jit(solution)/shard_map/ppermute | solution.py:30
  25.0 2.8 %shard_map.37 = (f32[8,32,384]{2,1,0:T(8,128)S(1)}, f32[8,32,384]{2,1,0:T(8,128)S(1)}) custom-call(bf16[24,32]{1,0:T(8,128)(2,1)S(1)} %get-tuple-element.15.refs_0_.refs_7_, bf16[24,32]{1,0:T(8,128)(2,1)S(1)} %collective-permute-done.4.refs_1_.refs_8_, bf16[48,32]{1,0:T(8,128)(2,1)S(1)} %collective-permute-done.5.refs_2_.refs_9_, ...), custom_call_target="tpu_custom_call" | custom-call | tf_op jit(solution)/shard_map/pallas_call | solution.py:181
  27.8 0.0 collective-permute-done.3.refs_4_
  27.8 2.6 %shard_map.38 = (f32[4,32,384]{2,1,0:T(8,128)S(1)}, f32[5,32,384]{2,1,0:T(8,128)S(1)}, bf16[8,256,128]{2,1,0:T(8,128)(2,1)S(1)}) custom-call(s32[1,2,384]{2,1,0:T(2,128)S(1)} %get-tuple-element.14.refs_0_, s32[1,2,384]{2,1,0:T(2,128)S(1)} %collective-permute-done.refs_1_, s32[2,2,384]{2,1,0:T(2,128)S(1)} %collective-permute-done.1.refs_2_, ...), custom_call_target="tpu_custom_call" | custom-call | tf_op jit(solution)/shard_map/pallas_call | solution.py:181
  30.4 2.5 %shard_map.39 = (f32[4,32,384]{2,1,0:T(8,128)S(1)}, f32[4,32,384]{2,1,0:T(8,128)S(1)}) custom-call(bf16[8,256,128]{2,1,0:T(8,128)(2,1)S(1)} %get-tuple-element.18.slots, bf16[24,32]{1,0:T(8,128)(2,1)S(1)} %get-tuple-element.15.refs_0_.refs_7_, bf16[24,32]{1,0:T(8,128)(2,1)S(1)} %collective-permute-done.4.refs_1_.refs_8_, ...), custom_call_target="tpu_custom_call" | custom-call | tf_op jit(solution)/shard_map/pallas_call | solution.py:181
  32.9 0.1 collective-permute-start.8
  33.0 0.5 collective-permute-start.12
  33.5 0.2 collective-permute-start.9
  33.7 0.7 %collective-permute-done.8 = f32[4,32,384]{2,1,0:T(8,128)S(1)} collective-permute-done((f32[4,32,384]{2,1,0:T(8,128)S(1)}, f32[4,32,384]{2,1,0:T(8,128)S(1)}, u32[]{:S(2)}, u32[]{:S(2)}) %collective-permute-start.8) | collective-permute-done | bytes 196640 | tf_op jit(solution)/shard_map/ppermute | solution.py:30
  34.4 0.3 collective-permute-done.12
  34.8 0.5 collective-permute-done.9
  35.5 0.6 %collective-permute-start.13 = (f16[144,384]{1,0:T(8,128)(2,1)S(1)}, f16[144,384]{1,0:T(8,128)(2,1)S(1)}, u32[]{:S(2)}, u32[]{:S(2)}) collective-permute-start(f16[144,384]{1,0:T(8,128)(2,1)S(1)} %pad_maximum_fusion), channel_id=1, source_target_pairs={{0,96},{16,112},{32,64},{48,80},{64,32},{80,48},{96,0},{112,16},{1... | collective-permute-start | bytes 331784 | tf_op jit(solution)/shard_map/ppermute | solution.py:30
  36.1 5.9 %collective-permute-done.13 = f16[144,384]{1,0:T(8,128)(2,1)S(1)} collective-permute-done((f16[144,384]{1,0:T(8,128)(2,1)S(1)}, f16[144,384]{1,0:T(8,128)(2,1)S(1)}, u32[]{:S(2)}, u32[]{:S(2)}) %collective-permute-start.13) | collective-permute-done | bytes 110624 | tf_op jit(solution)/shard_map/ppermute | solution.py:30
  42.2 0.1 collective-permute-start.14
  42.3 0.6 %collective-permute-start.10 = (f32[2,2,32,384]{3,2,1,0:T(8,128)S(1)}, f32[2,2,32,384]{3,2,1,0:T(8,128)S(1)}, u32[]{:S(2)}, u32[]{:S(2)}) collective-permute-start(f32[2,2,32,384]{3,2,1,0:T(8,128)S(1)} %copy.29), channel_id=1, source_target_pairs={{0,96},{16,112},{32,64},{48,80},{64,32},{80,48},{96,0},{112,16},{1... | collective-permute-start | bytes 589832 | tf_op jit(solution)/shard_map/ppermute | solution.py:30
  42.9 3.6 %collective-permute-done.14 = f16[80,384]{1,0:T(8,128)(2,1)S(1)} collective-permute-done((f16[80,384]{1,0:T(8,128)(2,1)S(1)}, f16[80,384]{1,0:T(8,128)(2,1)S(1)}, u32[]{:S(2)}, u32[]{:S(2)}) %collective-permute-start.14) | collective-permute-done | bytes 61472 | tf_op jit(solution)/shard_map/ppermute | solution.py:30
  46.6 1.0 %collective-permute-start.15 = (f16[80,384]{1,0:T(8,128)(2,1)S(1)}, f16[80,384]{1,0:T(8,128)(2,1)S(1)}, u32[]{:S(2)}, u32[]{:S(2)}) collective-permute-start(f16[80,384]{1,0:T(8,128)(2,1)S(1)} %pad_maximum_fusion.6), channel_id=1, source_target_pairs={{0,128},{16,144},{32,160},{48,176},{64,192},{80,208},{96,224},{112... | collective-permute-start | bytes 184328 | tf_op jit(solution)/shard_map/ppermute | solution.py:30
  47.6 2.2 %collective-permute-done.10 = f32[2,2,32,384]{3,2,1,0:T(8,128)S(1)} collective-permute-done((f32[2,2,32,384]{3,2,1,0:T(8,128)S(1)}, f32[2,2,32,384]{3,2,1,0:T(8,128)S(1)}, u32[]{:S(2)}, u32[]{:S(2)}) %collective-permute-start.10) | collective-permute-done | bytes 196640 | tf_op jit(solution)/shard_map/ppermute | solution.py:30
  49.8 0.6 %collective-permute-start.11 = (f32[2,32,384]{2,1,0:T(8,128)S(1)}, f32[2,32,384]{2,1,0:T(8,128)S(1)}, u32[]{:S(2)}, u32[]{:S(2)}) collective-permute-start(f32[2,32,384]{2,1,0:T(8,128)S(1)} %fusion.10), channel_id=1, source_target_pairs={{0,32},{16,48},{32,0},{48,16},{64,96},{80,112},{96,64},{112,80},{1... | collective-permute-start | bytes 294920 | tf_op jit(solution)/shard_map/ppermute | solution.py:30
  50.4 4.6 %collective-permute-done.15 = f16[80,384]{1,0:T(8,128)(2,1)S(1)} collective-permute-done((f16[80,384]{1,0:T(8,128)(2,1)S(1)}, f16[80,384]{1,0:T(8,128)(2,1)S(1)}, u32[]{:S(2)}, u32[]{:S(2)}) %collective-permute-start.15) | collective-permute-done | bytes 61472 | tf_op jit(solution)/shard_map/ppermute | solution.py:30
  55.1 0.0 collective-permute-done.11
  55.1 0.6 %pad_maximum_fusion.4 = f32[32,768]{1,0:T(8,128)} fusion(f32[32,384]{1,0:T(8,128)S(1)} %fusion.14, f32[32,384]{1,0:T(8,128)S(1)} %slice_bitcast_fusion.4), kind=kLoop, calls=%fused_computation.35 | loop fusion | flops 24576 | bytes 196608 | tf_op jit(solution)/shard_map/concatenate | solution.py:273
  (41 shorter events, 0.8 us)
Async XLA Ops:
  0.9 1.8 %collective-permute-start = (s32[1,2,384]{2,1,0:T(2,128)S(1)}, s32[1,2,384]{2,1,0:T(2,128)S(1)}, u32[]{:S(2)}, u32[]{:S(2)}) collective-permute-start(s32[1,2,384]{2,1,0:T(2,128)S(1)} %get-tuple-element.14.refs_0_), channel_id=1, source_target_pairs={{0,16},{16,0},{32,48},{48,32},{64,80},{80,64},{96,112},{112,96},{1... | collective-permute-start | bytes 9224 | tf_op jit(solution)/shard_map/ppermute | solution.py:30
  1.0 3.7 %collective-permute-start.4 = (bf16[24,32]{1,0:T(8,128)(2,1)S(1)}, bf16[24,32]{1,0:T(8,128)(2,1)S(1)}, u32[]{:S(2)}, u32[]{:S(2)}) collective-permute-start(bf16[24,32]{1,0:T(8,128)(2,1)S(1)} %get-tuple-element.15.refs_0_.refs_7_), channel_id=1, source_target_pairs={{0,4},{1,5},{2,6},{3,7},{4,0},{5,1},{6,2},{7,3},{8,12},{9,13},{10,... | collective-permute-start | bytes 4616 | tf_op jit(solution)/shard_map/ppermute | solution.py:30
  2.7 5.1 %collective-permute-start.1 = (s32[2,2,384]{2,1,0:T(2,128)S(1)}, s32[2,2,384]{2,1,0:T(2,128)S(1)}, u32[]{:S(2)}, u32[]{:S(2)}) collective-permute-start(s32[2,2,384]{2,1,0:T(2,128)S(1)} %pad_add_fusion.2), channel_id=1, source_target_pairs={{0,32},{16,48},{32,0},{48,16},{64,96},{80,112},{96,64},{112,80},{1... | collective-permute-start | bytes 18440 | tf_op jit(solution)/shard_map/ppermute | solution.py:30
  4.7 4.9 %collective-permute-start.5 = (bf16[48,32]{1,0:T(8,128)(2,1)S(1)}, bf16[48,32]{1,0:T(8,128)(2,1)S(1)}, u32[]{:S(2)}, u32[]{:S(2)}) collective-permute-start(bf16[48,32]{1,0:T(8,128)(2,1)S(1)} %pad_maximum_fusion.9), channel_id=1, source_target_pairs={{0,12},{1,13},{2,14},{3,15},{4,8},{5,9},{6,10},{7,11},{8,4},{9,5},... | collective-permute-start | bytes 9224 | tf_op jit(solution)/shard_map/ppermute | solution.py:30
  7.8 4.9 %collective-permute-start.2 = (s32[4,2,384]{2,1,0:T(2,128)S(1)}, s32[4,2,384]{2,1,0:T(2,128)S(1)}, u32[]{:S(2)}, u32[]{:S(2)}) collective-permute-start(s32[4,2,384]{2,1,0:T(2,128)S(1)} %pad_add_fusion.1), channel_id=1, source_target_pairs={{0,96},{16,112},{32,64},{48,80},{64,32},{80,48},{96,0},{112,16},{1... | collective-permute-start | bytes 36872 | tf_op jit(solution)/shard_map/ppermute | solution.py:30
  9.7 10.2 %collective-permute-start.6 = (bf16[96,32]{1,0:T(8,128)(2,1)S(1)}, bf16[96,32]{1,0:T(8,128)(2,1)S(1)}, u32[]{:S(2)}, u32[]{:S(2)}) collective-permute-start(bf16[96,32]{1,0:T(8,128)(2,1)S(1)} %pad_maximum_fusion.8), channel_id=1, source_target_pairs={{0,1},{1,0},{2,3},{3,2},{4,5},{5,4},{6,7},{7,6},{8,9},{9,8},{10,11... | collective-permute-start | bytes 18440 | tf_op jit(solution)/shard_map/ppermute | solution.py:30
  12.7 15.1 %collective-permute-start.3 = (s32[8,2,384]{2,1,0:T(2,128)S(1)}, s32[8,2,384]{2,1,0:T(2,128)S(1)}, u32[]{:S(2)}, u32[]{:S(2)}) collective-permute-start(s32[8,2,384]{2,1,0:T(2,128)S(1)} %pad_add_fusion), channel_id=1, source_target_pairs={{0,128},{16,144},{32,160},{48,176},{64,192},{80,208},{96,224},{112... | collective-permute-start | bytes 73736 | tf_op jit(solution)/shard_map/ppermute | solution.py:30
  19.9 5.1 %collective-permute-start.7 = (bf16[192,32]{1,0:T(8,128)(2,1)S(1)}, bf16[192,32]{1,0:T(8,128)(2,1)S(1)}, u32[]{:S(2)}, u32[]{:S(2)}) collective-permute-start(bf16[192,32]{1,0:T(8,128)(2,1)S(1)} %pad_maximum_fusion.7), channel_id=1, source_target_pairs={{0,2},{1,3},{2,0},{3,1},{4,6},{5,7},{6,4},{7,5},{8,10},{9,11},{10,... | collective-permute-start | bytes 36872 | tf_op jit(solution)/shard_map/ppermute | solution.py:30
  32.9 1.5 %collective-permute-start.8 = (f32[4,32,384]{2,1,0:T(8,128)S(1)}, f32[4,32,384]{2,1,0:T(8,128)S(1)}, u32[]{:S(2)}, u32[]{:S(2)}) collective-permute-start(f32[4,32,384]{2,1,0:T(8,128)S(1)} %get-tuple-element.20), channel_id=1, source_target_pairs={{0,16},{16,0},{32,48},{48,32},{64,80},{80,64},{96,112},{112,96},{1... | collective-permute-start | bytes 589832 | tf_op jit(solution)/shard_map/ppermute | solution.py:30
  33.0 1.8 %collective-permute-start.12 = (f32[5,32,384]{2,1,0:T(8,128)S(1)}, f32[5,32,384]{2,1,0:T(8,128)S(1)}, u32[]{:S(2)}, u32[]{:S(2)}) collective-permute-start(f32[5,32,384]{2,1,0:T(8,128)S(1)} %get-tuple-element.22), channel_id=1, source_target_pairs={{0,16},{16,0},{32,48},{48,32},{64,80},{80,64},{96,112},{112,96},{1... | collective-permute-start | bytes 737288 | tf_op jit(solution)/shard_map/ppermute | solution.py:30
  33.5 1.8 %collective-permute-start.9 = (f32[8,32,384]{2,1,0:T(8,128)S(1)}, f32[8,32,384]{2,1,0:T(8,128)S(1)}, u32[]{:S(2)}, u32[]{:S(2)}) collective-permute-start(f32[8,32,384]{2,1,0:T(8,128)S(1)} %get-tuple-element.17.refs_6_), channel_id=1, source_target_pairs={{0,16},{16,0},{32,48},{48,32},{64,80},{80,64},{96,112},{112,96},{1... | collective-permute-start | bytes 1179656 | tf_op jit(solution)/shard_map/ppermute | solution.py:30
  35.5 6.5 %collective-permute-start.13 = (f16[144,384]{1,0:T(8,128)(2,1)S(1)}, f16[144,384]{1,0:T(8,128)(2,1)S(1)}, u32[]{:S(2)}, u32[]{:S(2)}) collective-permute-start(f16[144,384]{1,0:T(8,128)(2,1)S(1)} %pad_maximum_fusion), channel_id=1, source_target_pairs={{0,96},{16,112},{32,64},{48,80},{64,32},{80,48},{96,0},{112,16},{1... | collective-permute-start | bytes 331784 | tf_op jit(solution)/shard_map/ppermute | solution.py:30
  42.2 4.3 %collective-permute-start.14 = (f16[80,384]{1,0:T(8,128)(2,1)S(1)}, f16[80,384]{1,0:T(8,128)(2,1)S(1)}, u32[]{:S(2)}, u32[]{:S(2)}) collective-permute-start(f16[80,384]{1,0:T(8,128)(2,1)S(1)} %pad_maximum_fusion.5), channel_id=1, source_target_pairs={{0,32},{16,48},{32,0},{48,16},{64,96},{80,112},{96,64},{112,80},{1... | collective-permute-start | bytes 184328 | tf_op jit(solution)/shard_map/ppermute | solution.py:30
  42.3 7.5 %collective-permute-start.10 = (f32[2,2,32,384]{3,2,1,0:T(8,128)S(1)}, f32[2,2,32,384]{3,2,1,0:T(8,128)S(1)}, u32[]{:S(2)}, u32[]{:S(2)}) collective-permute-start(f32[2,2,32,384]{3,2,1,0:T(8,128)S(1)} %copy.29), channel_id=1, source_target_pairs={{0,96},{16,112},{32,64},{48,80},{64,32},{80,48},{96,0},{112,16},{1... | collective-permute-start | bytes 589832 | tf_op jit(solution)/shard_map/ppermute | solution.py:30
  46.6 8.4 %collective-permute-start.15 = (f16[80,384]{1,0:T(8,128)(2,1)S(1)}, f16[80,384]{1,0:T(8,128)(2,1)S(1)}, u32[]{:S(2)}, u32[]{:S(2)}) collective-permute-start(f16[80,384]{1,0:T(8,128)(2,1)S(1)} %pad_maximum_fusion.6), channel_id=1, source_target_pairs={{0,128},{16,144},{32,160},{48,176},{64,192},{80,208},{96,224},{112... | collective-permute-start | bytes 184328 | tf_op jit(solution)/shard_map/ppermute | solution.py:30
  49.8 5.3 %collective-permute-start.11 = (f32[2,32,384]{2,1,0:T(8,128)S(1)}, f32[2,32,384]{2,1,0:T(8,128)S(1)}, u32[]{:S(2)}, u32[]{:S(2)}) collective-permute-start(f32[2,32,384]{2,1,0:T(8,128)S(1)} %fusion.10), channel_id=1, source_target_pairs={{0,32},{16,48},{32,0},{48,16},{64,96},{80,112},{96,64},{112,80},{1... | collective-permute-start | bytes 294920 | tf_op jit(solution)/shard_map/ppermute | solution.py:30
